TPU v7x, 32 devices: a whole 2x2x4 slice. The times are simulated.
32 devices in a mesh: section: 2 (over core), expert: 16 (over z, y, x).
Axes of the slice: x: 2, y: 2, z: 4, core: 2. Of those that a mesh axis runs over, the one named last changes fastest.
Arguments:
- tokens: bfloat16 [2, 2048, 2048], P('section', 'expert'), may hold values from -6 to 6
- cotangent: bfloat16 [2, 2048, 2048], P('section', 'expert'), may hold values from -3 to 3
- routes: int32 [2, 2048, 8], P('section', 'expert'), may hold values from 0 to 15, all different within a row; in each aligned block of 128 rows (0 to 127, 128 to 255, ..., all dimensions but the last counted through in order) at most 72 rows name the same one
- route_weights: bfloat16 [2, 2048, 8], P('section', 'expert'), may hold values from 0.099609375 to 1
- weights: bfloat16 [3, 16, 2048, 384], P(None, 'expert'), may hold values from -0.125 to 0.125
Outputs:
- token_grads: bfloat16 [2, 2048, 2048], P('section', 'expert')
- gate_grads: bfloat16 [2, 2048, 8], P('section', 'expert')
- weight_grads: float32 [3, 16, 2048, 384], P(None, 'expert', 'section')
Inputs may be any that keep to these rules, and one draw needn't show every extreme that they name: `routes`: the 8 experts of a token differ. Among the 128 tokens of one device no expert is named more than 72 times, a bound that some block reaches.
All inputs are finite; a program needn't handle non-finite values.
Results may differ from a plain program's by a relative error of at most 0.0085.
Values may be sent and summed in bfloat16 or wider, within the bound.
A program may use at most 128 MiB of HBM per device.

v0:
```python
import functools

import jax
import jax.numpy as jnp
from jax import lax
from jax.experimental import pallas as pl
from jax.experimental.pallas import tpu as pltpu
from jax.sharding import PartitionSpec as P

MESH = pl.DeviceIdType.MESH
LANES = 128
ROW_TILE = 16


def slot_assign(route_block, experts, capacity):
    flat_ids = route_block.reshape(-1)
    pair_count = flat_ids.shape[0]
    one_hot = (flat_ids[:, None] == jnp.arange(experts, dtype=jnp.int32)[None, :]).astype(jnp.int32)
    before = jnp.cumsum(one_hot, axis=0) - one_hot
    slot_of = jnp.sum(before * one_hot, axis=1)
    slot_table = jnp.full((experts, capacity), pair_count, jnp.int32)
    slot_table = slot_table.at[flat_ids, slot_of].set(jnp.arange(pair_count, dtype=jnp.int32))
    return (slot_of.reshape(route_block.shape), slot_table)


def expert_math(in_rows, cot_rows, weight, expert_w):
    f32 = jnp.float32
    gate_pre = jnp.dot(in_rows, expert_w[0], preferred_element_type=f32)
    up_pre = jnp.dot(in_rows, expert_w[1], preferred_element_type=f32)
    sigmoid_v = jax.nn.sigmoid(gate_pre)
    silu_v = gate_pre * sigmoid_v
    hidden = (silu_v * up_pre).astype(jnp.bfloat16)
    back_proj = jnp.dot(cot_rows, expert_w[2], preferred_element_type=f32)
    row_gate = jnp.sum(hidden.astype(f32) * back_proj, axis=1).astype(jnp.bfloat16)
    weight = weight.astype(f32)[:, None]
    d_hidden = weight * back_proj
    d_gate_pre = (d_hidden * up_pre * sigmoid_v * (1.0 + gate_pre * (1.0 - sigmoid_v))).astype(
        jnp.bfloat16
    )
    d_up_pre = (d_hidden * silu_v).astype(jnp.bfloat16)
    scaled = (weight * cot_rows.astype(f32)).astype(jnp.bfloat16)
    rows = (((0,), (0,)), ((), ()))
    weight_part = jnp.stack(
        [
            lax.dot_general(in_rows, d_gate_pre, rows, preferred_element_type=f32),
            lax.dot_general(in_rows, d_up_pre, rows, preferred_element_type=f32),
            lax.dot_general(scaled, hidden, rows, preferred_element_type=f32),
        ]
    )
    ff = (((1,), (1,)), ((), ()))
    row_grads = (
        lax.dot_general(d_gate_pre, expert_w[0], ff, preferred_element_type=f32)
        + lax.dot_general(d_up_pre, expert_w[1], ff, preferred_element_type=f32)
    ).astype(jnp.bfloat16)
    return (row_gate, row_grads, weight_part)


def section_mean(weight_part):
    partial_sum = weight_part[:, None].astype(jnp.bfloat16)
    sections = lax.axis_size("section")
    share = lax.psum_scatter(partial_sum, "section", scatter_dimension=2, tiled=True)
    return share.astype(jnp.float32) / sections


def line_order(count):
    order, low, high = [], 0, count - 1
    while low <= high:
        order.append(high)
        if low < high:
            order.append(low)
        low, high = low + 1, high - 1
    return order


def pick(table, index):
    value = table[0]
    for place in range(1, len(table)):
        value = jnp.where(index == place, table[place], value)
    return value


def fused_kernel(
    experts, split, gather_parts, x_hbm, c_hbm, w_hbm, weights_hbm,
    tok_out, gate_out, own_out, other_out,
    xc, part_g, wgu, wdn, dgu, whid, wsend, wrecv, wown, rq, rz_a, rz_b, rp_a, rp_b,
    loc_sem, bs_sem, br_sem, qs_sem, qr_sem, zs_sem, zr_sem, ps_sem, pr_sem, ws_sem, wr_sem, out_sem,
):
    f32, bf16 = jnp.float32, jnp.bfloat16
    z_count = experts // 4
    tok, depth = x_hbm.shape
    ff = weights_hbm.shape[2]
    sec = lax.axis_index("section")
    me = lax.axis_index("expert")
    z, yb, xb = me // 4, (me // 2) % 2, me % 2
    p_unit, q_unit = 2 - sec, 1 + sec
    pv = yb * (1 - sec) + xb * sec
    qv = xb * (1 - sec) + yb * sec
    peers = {
        "up": {"expert": me + 4},
        "down": {"expert": me - 4},
        "p": {"expert": me + p_unit * (1 - 2 * pv)},
        "q": {"expert": me + q_unit * (1 - 2 * qv)},
        "sec": {"section": 1 - sec},
    }
    has = {"up": z < z_count - 1, "down": z > 0, "p": None, "q": None, "sec": None}
    dirs = {"up": 0, "down": 1, "p": 2, "q": 3}
    order_z = line_order(z_count)

    def when(*conds):
        conds = [cond for cond in conds if cond is not None]
        if not conds:
            return lambda body: body()
        joined = conds[0]
        for cond in conds[1:]:
            joined = joined & cond
        return pl.when(joined)

    def slot_of(fp, fq, zz):
        return (p_unit * ((pv + fp) % 2) + q_unit * ((qv + fq) % 2)) * z_count + zz

    own = slot_of(0, 0, z)
    local = [
        pltpu.make_async_copy(x_hbm, xc.at[own, :, pl.ds(0, depth)], loc_sem.at[0]),
        pltpu.make_async_copy(c_hbm, xc.at[own, :, pl.ds(depth, depth)], loc_sem.at[1]),
        pltpu.make_async_copy(w_hbm, xc.at[own, :, pl.ds(2 * depth, LANES)], loc_sem.at[2]),
        pltpu.make_async_copy(weights_hbm.at[0], wgu.at[:, pl.ds(0, ff)], loc_sem.at[3]),
        pltpu.make_async_copy(weights_hbm.at[1], wgu.at[:, pl.ds(ff, ff)], loc_sem.at[4]),
        pltpu.make_async_copy(weights_hbm.at[2], wdn, loc_sem.at[5]),
    ]
    for copy in local:
        copy.start()

    barrier = pltpu.get_barrier_semaphore()
    for name, peer in peers.items():
        @when(has[name])
        def _(peer=peer):
            pl.semaphore_signal(barrier, inc=1, device_id=peer, device_id_type=MESH)
    pl.semaphore_wait(barrier, 3 + jnp.where(has["up"], 1, 0) + jnp.where(has["down"], 1, 0))

    for copy in local[:3]:
        copy.wait()

    halves = ((0, split), (split, tok - split))
    sent = []

    def block_copy(part, slot, name):
        start, rows = gather_parts[part]
        view = xc.at[slot, pl.ds(start, rows)]
        return pltpu.make_async_remote_copy(
            src_ref=view,
            dst_ref=view,
            send_sem=bs_sem.at[part, dirs[name], slot],
            recv_sem=br_sem.at[part, slot],
            device_id=peers[name],
            device_id_type=MESH,
        )

    def forward(part, fp, dz, names):
        slot = slot_of(fp, 0, z + dz)
        valid = None if dz == 0 else ((z + dz >= 0) & (z + dz < z_count))
        for name in names:
            @when(valid, has[name])
            def _(name=name):
                block_copy(part, slot, name).start()
            sent.append((part, slot, name, valid))

    def arrive(part, fp, fq, dz):
        slot = slot_of(fp, fq, z + dz)
        valid = None if dz == 0 else ((z + dz >= 0) & (z + dz < z_count))

        @when(valid)
        def _():
            block_copy(part, slot, "q").wait_recv()

    late = range(1, len(gather_parts))
    for part in late:
        forward(part, 0, 0, ("p", "q", "up", "down"))
    forward(0, 0, 0, ("up", "down", "p", "q"))
    for part in late:
        arrive(part, 1, 0, 0)
        forward(part, 1, 0, ("up", "down", "q"))
    pending = [0]
    for step in range(1, z_count):
        for dz in (-step, step):
            onward = "up" if dz < 0 else "down"
            arrive(0, 0, 0, dz)
            forward(0, 0, dz, (onward, "p", "q"))
        for fp in (0, 1):
            for part in late:
                for dz in (-step, step):
                    onward = "up" if dz < 0 else "down"
                    arrive(part, fp, 0, dz)
                    forward(part, fp, dz, (onward, "q"))
        for dz in pending:
            arrive(0, 1, 0, dz)
            forward(0, 1, dz, ("q",))
        pending = [-step, step]
    for dz in pending:
        arrive(0, 1, 0, dz)
        forward(0, 1, dz, ("q",))
    for copy in local[3:]:
        copy.wait()

    lane = lax.broadcasted_iota(jnp.int32, (1, LANES), 1)
    pair = 2
    rows_step = pair * tok

    def q_copy(fp, place, slot):
        return pltpu.make_async_remote_copy(
            src_ref=part_g.at[slot],
            dst_ref=rq.at[place],
            send_sem=qs_sem.at[place],
            recv_sem=qr_sem.at[place],
            device_id=peers["q"],
            device_id_type=MESH,
        )

    def batch(number, carry):
        fq = number // 2
        fp = number % 2
        base = slot_of(fp, fq, 0)

        @pl.when(fq == 1)
        def _():
            for zz in range(z_count):
                for part in range(len(gather_parts)):
                    block_copy(part, base + zz, "q").wait_recv()

        def tile(half, inner):
            slot = base + half * pair
            x = xc[pl.ds(slot, pair), :, pl.ds(0, depth)].reshape(rows_step, depth)
            c = xc[pl.ds(slot, pair), :, pl.ds(depth, depth)].reshape(rows_step, depth)
            w = xc[pl.ds(slot, pair), :, pl.ds(2 * depth, LANES)].reshape(rows_step, LANES)
            weight = jnp.sum(jnp.where(lane == me, w.astype(f32), 0.0), axis=1, keepdims=True)
            gu = jnp.dot(x, wgu[...], preferred_element_type=f32)
            back = jnp.dot(c, wdn[...], preferred_element_type=f32)
            gate, up = gu[:, :ff], gu[:, ff:]
            sig = jax.nn.sigmoid(gate)
            silu = gate * sig
            hid = silu * up
            row_gate = jnp.sum(hid * back, axis=1, keepdims=True)
            d_hid = weight * back
            d_gate = (d_hid * up * sig * (1.0 + gate * (1.0 - sig))).astype(bf16)
            d_up = (d_hid * silu).astype(bf16)
            rows = pl.ds(pl.multiple_of(slot * tok, rows_step), rows_step)
            dgu[rows, pl.ds(0, ff)] = d_gate
            dgu[rows, pl.ds(ff, ff)] = d_up
            whid[rows, :] = (weight * hid).astype(bf16)
            grads = lax.dot_general(
                dgu[rows, :], wgu[...], (((1,), (1,)), ((), ())), preferred_element_type=f32
            )
            part_g[pl.ds(slot, pair), :, pl.ds(0, depth)] = grads.astype(bf16).reshape(pair, tok, depth)
            marked = jnp.where(lane == me, row_gate, 0.0).astype(bf16)
            part_g[pl.ds(slot, pair), :, pl.ds(depth, LANES)] = marked.reshape(pair, tok, LANES)
            return inner

        lax.fori_loop(0, z_count // pair, tile, 0)

        return carry

    lax.fori_loop(0, 4, batch, 0)
    for fp in (1, 0):
        for place, zz in enumerate(order_z):
            q_copy(fp, (1 - fp) * z_count + place, slot_of(fp, 1, zz)).start()

    def add_rows(slot, start, rows, view):
        def strip(k, carry):
            at = pl.ds(pl.multiple_of(start + k * ROW_TILE, ROW_TILE), ROW_TILE)
            off = pl.ds(pl.multiple_of(k * ROW_TILE, ROW_TILE), ROW_TILE)
            total = part_g[slot, at, :].astype(f32) + view[off, :].astype(f32)
            part_g[slot, at, :] = total.astype(bf16)
            return carry

        lax.fori_loop(0, rows // ROW_TILE, strip, 0)

    def p_copy(part, zz, slot):
        start, rows = halves[part]
        place = zz if part == 0 else z_count
        return pltpu.make_async_remote_copy(
            src_ref=part_g.at[slot, pl.ds(start, rows)],
            dst_ref=rp_a.at[zz] if part == 0 else rp_b,
            send_sem=ps_sem.at[place],
            recv_sem=pr_sem.at[place],
            device_id=peers["p"],
            device_id_type=MESH,
        )

    groups = ((0, 0, rz_a), (1, 0, rz_b.at[0]), (1, 1, rz_b.at[1]))

    def z_copy(group, dest, name, place):
        part, fp, buf = groups[group]
        start, rows = halves[part]
        return pltpu.make_async_remote_copy(
            src_ref=part_g.at[slot_of(fp, 0, dest), pl.ds(start, rows)],
            dst_ref=buf.at[place],
            send_sem=zs_sem.at[group, dest],
            recv_sem=zr_sem.at[group, place],
            device_id=peers[name],
            device_id_type=MESH,
        )

    def z_take(group, dest, place):
        part, fp, buf = groups[group]
        start, rows = halves[part]
        z_copy(group, 0, "p", place).wait_recv()
        add_rows(slot_of(fp, 0, dest), start, rows, buf.at[place])

    def z_send(group, dest):
        @pl.when(z < dest)
        def _():
            z_copy(group, dest, "up", dest).start()

        @pl.when(z > dest)
        def _():
            z_copy(group, dest, "down", jnp.where(z == dest + 1, z_count, dest)).start()

    def relays(dest):
        return ((z < dest) & (z > 0)) | ((z > dest) & (z < z_count - 1))

    def z_origin(group, dest):
        @pl.when(jnp.logical_not(relays(dest)))
        def _():
            z_send(group, dest)

    def z_relay(group, dest):
        @pl.when(relays(dest))
        def _():
            z_take(group, dest, dest)
            z_send(group, dest)

    def z_own(group):
        @pl.when(z > 0)
        def _():
            z_take(group, z, z)

        @pl.when(z < z_count - 1)
        def _():
            z_take(group, z, z_count)

    chunks = z_count
    width = wsend.shape[1] // chunks

    def chunk_rows(k):
        return pl.ds(pl.multiple_of(k * width, width), width)

    def out_copies(k):
        at = chunk_rows(k)
        return (
            pltpu.make_async_copy(wown.at[:, at, :], own_out.at[:, at, :], out_sem.at[0, k]),
            pltpu.make_async_copy(wrecv.at[:, at, :], other_out.at[:, at, :], out_sem.at[1, k]),
        )

    def w_copy(k):
        return pltpu.make_async_remote_copy(
            src_ref=wsend.at[:, chunk_rows(k), :],
            dst_ref=wrecv.at[:, chunk_rows(k), :],
            send_sem=ws_sem.at[k],
            recv_sem=wr_sem.at[k],
            device_id=peers["sec"],
            device_id_type=MESH,
        )

    fold = (((0,), (0,)), ((), ()))

    def returned(i, carry):
        fp = 1 - i // z_count
        zz = pick(order_z, i % z_count)
        slot = slot_of(fp, 0, zz)
        away = i < chunks
        half = jnp.where(away, 1 - sec, sec)
        col = (half * chunks + i % chunks) * width
        xs = xc[:, :, pl.ds(pl.multiple_of(col, width), width)].reshape(-1, width)
        cs = xc[:, :, pl.ds(pl.multiple_of(depth + col, width), width)].reshape(-1, width)
        got_gu = lax.dot_general(xs, dgu[...], fold, preferred_element_type=f32).astype(bf16)
        got_dn = lax.dot_general(cs, whid[...], fold, preferred_element_type=f32).astype(bf16)

        @pl.when(away)
        def _():
            k = i % chunks
            wsend[0, chunk_rows(k), :] = got_gu[:, :ff]
            wsend[1, chunk_rows(k), :] = got_gu[:, ff:]
            wsend[2, chunk_rows(k), :] = got_dn
            w_copy(k).start()

        @pl.when(jnp.logical_not(away))
        def _():
            k = i % chunks
            wown[0, chunk_rows(k), :] = got_gu[:, :ff]
            wown[1, chunk_rows(k), :] = got_gu[:, ff:]
            wown[2, chunk_rows(k), :] = got_dn
            w_copy(k).wait_recv()
            for copy in out_copies(k):
                copy.start()

        before = pick(order_z, (i + z_count - 1) % z_count)

        @pl.when((i >= 1) & (i <= z_count))
        def _():
            z_relay(2, before)

        @pl.when(i > z_count)
        def _():
            z_relay(1, before)
            z_relay(0, before)

        q_copy(fp, i, slot).wait_recv()
        add_rows(slot, 0, tok, rq.at[i])

        @pl.when(fp == 1)
        def _():
            p_copy(0, zz, slot).start()
            z_origin(2, zz)

        @pl.when(fp == 0)
        def _():
            z_origin(1, zz)
            p_copy(0, zz, slot).wait_recv()
            add_rows(slot, 0, split, rp_a.at[zz])
            z_origin(0, zz)

        @pl.when(i == 2 * z_count - 2)
        def _():
            z_own(2)
            p_copy(1, z, slot_of(1, 0, z)).start()

        return carry

    lax.fori_loop(0, 2 * z_count, returned, 0)

    last = order_z[-1]
    z_relay(1, last)
    z_relay(0, last)
    p_copy(1, z, own).wait_recv()
    add_rows(own, split, tok - split, rp_b)
    z_own(1)
    z_own(0)
    tok_out[...] = part_g[own, :, pl.ds(0, depth)]
    gate_out[...] = part_g[own, :, pl.ds(depth, LANES)]

    for k in range(chunks):
        w_copy(k).wait_send()
        for copy in out_copies(k):
            copy.wait()
    for part, slot, name, valid in sent:
        @when(valid, has[name])
        def _(part=part, slot=slot, name=name):
            block_copy(part, slot, name).wait_send()
    for place in range(2 * z_count):
        q_copy(0, place, own).wait_send()
    for zz in range(z_count):
        p_copy(0, zz, own).wait_send()
    p_copy(1, z, own).wait_send()
    for group in range(3):
        for dest in range(z_count):
            @pl.when(z != dest)
            def _():
                z_copy(group, dest, "p", dest).wait_send()


def gathered(tokens, cotangent, routes, route_weights, weights):
    experts = lax.axis_size("expert")
    sections = lax.axis_size("section")
    z_count = experts // 4
    tok, depth = tokens.shape[1:]
    ff = weights.shape[3]
    named = routes[0][:, :, None] == jnp.arange(LANES, dtype=jnp.int32)
    dense_w = jnp.sum(jnp.where(named, route_weights[0][:, :, None], 0), axis=1)
    unit = tok // 8 // ROW_TILE * ROW_TILE
    split = tok // 2 // ROW_TILE * ROW_TILE
    gather_parts = ((0, 4 * unit), (4 * unit, 2 * unit), (6 * unit, tok - 6 * unit))
    bf16 = jnp.bfloat16
    g_width = depth + LANES
    chunks = z_count
    share = depth // sections
    dma = pltpu.SemaphoreType.DMA
    any_spec = pl.BlockSpec(memory_space=pl.ANY)
    vmem_spec = pl.BlockSpec(memory_space=pltpu.VMEM)
    token_grads, gates, own_part, other_part = pl.pallas_call(
        functools.partial(fused_kernel, experts, split, gather_parts),
        out_shape=(
            jax.ShapeDtypeStruct((tok, depth), bf16),
            jax.ShapeDtypeStruct((tok, LANES), bf16),
            jax.ShapeDtypeStruct((3, share, ff), bf16),
            jax.ShapeDtypeStruct((3, share, ff), bf16),
        ),
        in_specs=[any_spec] * 4,
        out_specs=(vmem_spec, vmem_spec, any_spec, any_spec),
        scratch_shapes=[
            pltpu.VMEM((experts, tok, 2 * depth + LANES), bf16),
            pltpu.VMEM((experts, tok, g_width), bf16),
            pltpu.VMEM((depth, 2 * ff), bf16),
            pltpu.VMEM((depth, ff), bf16),
            pltpu.VMEM((experts * tok, 2 * ff), bf16),
            pltpu.VMEM((experts * tok, ff), bf16),
            pltpu.VMEM((3, share, ff), bf16),
            pltpu.VMEM((3, share, ff), bf16),
            pltpu.VMEM((3, share, ff), bf16),
            pltpu.VMEM((2 * z_count, tok, g_width), bf16),
            pltpu.VMEM((z_count + 1, split, g_width), bf16),
            pltpu.VMEM((2, z_count + 1, tok - split, g_width), bf16),
            pltpu.VMEM((z_count, split, g_width), bf16),
            pltpu.VMEM((tok - split, g_width), bf16),
            dma((6,)),
            dma((len(gather_parts), 4, experts)),
            dma((len(gather_parts), experts)),
            dma((2 * z_count,)),
            dma((2 * z_count,)),
            dma((3, z_count)),
            dma((3, z_count + 1)),
            dma((z_count + 1,)),
            dma((z_count + 1,)),
            dma((chunks,)),
            dma((chunks,)),
            dma((2, chunks)),
        ],
        compiler_params=pltpu.CompilerParams(
            collective_id=0, has_side_effects=True, vmem_limit_bytes=67043328
        ),
    )(tokens[0], cotangent[0], dense_w, weights[:, 0])
    gate_grads = jnp.sum(jnp.where(named, gates[:, None, :], 0), axis=2)[None]
    weight_grads = (own_part.astype(jnp.float32) + other_part.astype(jnp.float32)) / sections
    return (token_grads[None], gate_grads, weight_grads[:, None])


def exchanged(tokens, cotangent, routes, route_weights, weights):
    experts = lax.axis_size("expert")
    tok_count, depth = tokens.shape[1:]
    top_k = routes.shape[-1]
    capacity = min(tok_count, max(2, (9 * tok_count * top_k + 8 * experts - 1) // (8 * experts)))
    route_block = routes[0]
    slots, slot_table = slot_assign(route_block, experts, capacity)
    token_ix = slot_table // top_k
    zero_row = jnp.zeros((1, depth), tokens.dtype)
    send_in = jnp.concatenate([tokens[0], zero_row])[token_ix]
    send_cot = jnp.concatenate([cotangent[0], zero_row])[token_ix]
    send_weight = jnp.concatenate(
        [route_weights[0].reshape(-1), jnp.zeros((1,), route_weights.dtype)]
    )[slot_table]
    recv_in, recv_cot, recv_weight = (
        lax.all_to_all(block, "expert", split_axis=0, concat_axis=0, tiled=True)
        for block in (send_in, send_cot, send_weight)
    )
    row_gate, row_grads, weight_part = expert_math(
        recv_in.reshape(-1, depth), recv_cot.reshape(-1, depth), recv_weight.reshape(-1), weights[:, 0]
    )
    back_rows, back_gate = (
        lax.all_to_all(block, "expert", split_axis=0, concat_axis=0, tiled=True)
        for block in (
            row_grads.reshape(experts, capacity, depth),
            row_gate.reshape(experts, capacity),
        )
    )
    flat_rows = back_rows.reshape(experts * capacity, depth)
    flat_index = route_block * capacity + slots
    accum = jnp.zeros((tok_count, depth), jnp.float32)
    for position in range(top_k):
        accum = accum + flat_rows[flat_index[:, position]].astype(jnp.float32)
    token_grads = accum.astype(jnp.bfloat16)[None]
    gate_grads = back_gate.reshape(-1)[flat_index][None]
    return (token_grads, gate_grads, section_mean(weight_part))


def solution(mesh):
    placed = P("section", "expert", None)

    def per_device(tokens, cotangent, routes, route_weights, weights):
        dense = 4 * routes.shape[-1] >= lax.axis_size("expert")
        plan = gathered if dense else exchanged
        return plan(tokens, cotangent, routes, route_weights, weights)

    return jax.shard_map(
        per_device,
        mesh=mesh,
        in_specs=(placed, placed, placed, placed, P(None, "expert", None, None)),
        out_specs=(placed, placed, P(None, "expert", "section", None)),
        check_vma=False,
    )
```

profile of v0, /device:TPU:8, one launch (start us, length us, event | category | flops | bytes accessed | tf_op | source)
XLA Modules:
  0.0 240.9 jit_solution(18411554449693803773)
XLA Ops:
  0.6 0.8 copy.12
  1.4 0.8 copy.11
  2.2 0.0 copy-start
  2.2 0.6 copy-done
  2.8 1.0 fusion.2.w_hbm
  3.8 229.2 %shard_map.76 = (bf16[128,2048]{1,0:T(8,128)(2,1)}, bf16[128,128]{1,0:T(8,128)(2,1)}, bf16[3,1024,384]{2,1,0:T(8,128)(2,1)}, bf16[3,1024,384]{2,1,0:T(8,128)(2,1)}) custom-call(bf16[128,2048]{1,0:T(8,128)(2,1)} %bitcast.13, bf16[128,2048]{1,0:T(8,128)(2,1)} %bitcast.14, bf16[128,128]{1,0:T(8,128)(2,1)} %fusion.2.w_hbm, bf16[3,2048,384]{2,1,0:T(8,128)(2,1)} %bitcast.11), custom_call_target="tpu_custom_call" | custom-call | tf_op jit(solution)/shard_map/pallas_call | solution.py:478
  233.0 1.2 fusion.3
  234.2 0.7 copy.13
  234.9 0.0 copy-start.1
  234.9 5.2 %multiply_bitcast_fusion = f32[3,1,1024,384]{3,2,1,0:T(8,128)} fusion(bf16[3,1024,384]{2,1,0:T(8,128)(2,1)} %get-tuple-element.10, bf16[3,1024,384]{2,1,0:T(8,128)(2,1)} %get-tuple-element.9), kind=kLoop, calls=%fused_computation | loop fusion | flops 4718592 | bytes 9437184
  240.1 0.0 copy-done.1
  240.1 0.8 copy.16
Async XLA Ops:
  2.2 0.6 copy-start
  234.9 5.2 %copy-start.1 = (bf16[128,2048]{1,0:T(8,128)(2,1)S(1)}, bf16[128,2048]{1,0:T(8,128)(2,1)}, u32[]{:S(2)}) copy-start(bf16[128,2048]{1,0:T(8,128)(2,1)} %get-tuple-element.7) | copy-start | bytes 1572868
where the time goes:
time: 241 us
  Pallas kernels  229 us (95%)
  other arithmetic  7.42 us (3%)
  local copies, waits for them, and re-layouts  3.66 us (2%)
    pallas_call x1, Pallas kernels, gathered(): pl.pallas_call(functools.partial(fused_kernel, experts, split, gather_par...  229 us
    unnamed x1, other arithmetic  5.23 us

commit v1 on v0

v1 whole, which is shorter than its diff:
```python
import functools

import jax
import jax.numpy as jnp
from jax import lax
from jax.experimental import pallas as pl
from jax.experimental.pallas import tpu as pltpu
from jax.sharding import PartitionSpec as P

MESH = pl.DeviceIdType.MESH
LANES = 128
ROW_TILE = 16


def slot_assign(route_block, experts, capacity):
    flat_ids = route_block.reshape(-1)
    pair_count = flat_ids.shape[0]
    one_hot = (flat_ids[:, None] == jnp.arange(experts, dtype=jnp.int32)[None, :]).astype(jnp.int32)
    before = jnp.cumsum(one_hot, axis=0) - one_hot
    slot_of = jnp.sum(before * one_hot, axis=1)
    slot_table = jnp.full((experts, capacity), pair_count, jnp.int32)
    slot_table = slot_table.at[flat_ids, slot_of].set(jnp.arange(pair_count, dtype=jnp.int32))
    return (slot_of.reshape(route_block.shape), slot_table)


def expert_math(in_rows, cot_rows, weight, expert_w):
    f32 = jnp.float32
    gate_pre = jnp.dot(in_rows, expert_w[0], preferred_element_type=f32)
    up_pre = jnp.dot(in_rows, expert_w[1], preferred_element_type=f32)
    sigmoid_v = jax.nn.sigmoid(gate_pre)
    silu_v = gate_pre * sigmoid_v
    hidden = (silu_v * up_pre).astype(jnp.bfloat16)
    back_proj = jnp.dot(cot_rows, expert_w[2], preferred_element_type=f32)
    row_gate = jnp.sum(hidden.astype(f32) * back_proj, axis=1).astype(jnp.bfloat16)
    weight = weight.astype(f32)[:, None]
    d_hidden = weight * back_proj
    d_gate_pre = (d_hidden * up_pre * sigmoid_v * (1.0 + gate_pre * (1.0 - sigmoid_v))).astype(
        jnp.bfloat16
    )
    d_up_pre = (d_hidden * silu_v).astype(jnp.bfloat16)
    scaled = (weight * cot_rows.astype(f32)).astype(jnp.bfloat16)
    rows = (((0,), (0,)), ((), ()))
    weight_part = jnp.stack(
        [
            lax.dot_general(in_rows, d_gate_pre, rows, preferred_element_type=f32),
            lax.dot_general(in_rows, d_up_pre, rows, preferred_element_type=f32),
            lax.dot_general(scaled, hidden, rows, preferred_element_type=f32),
        ]
    )
    ff = (((1,), (1,)), ((), ()))
    row_grads = (
        lax.dot_general(d_gate_pre, expert_w[0], ff, preferred_element_type=f32)
        + lax.dot_general(d_up_pre, expert_w[1], ff, preferred_element_type=f32)
    ).astype(jnp.bfloat16)
    return (row_gate, row_grads, weight_part)


def section_mean(weight_part):
    partial_sum = weight_part[:, None].astype(jnp.bfloat16)
    sections = lax.axis_size("section")
    share = lax.psum_scatter(partial_sum, "section", scatter_dimension=2, tiled=True)
    return share.astype(jnp.float32) / sections


def line_order(count):
    order, low, high = [], 0, count - 1
    while low <= high:
        order.append(high)
        if low < high:
            order.append(low)
        low, high = low + 1, high - 1
    return order


def pick(table, index):
    value = table[0]
    for place in range(1, len(table)):
        value = jnp.where(index == place, table[place], value)
    return value


def fused_kernel(
    experts, split, cuts, x_hbm, c_hbm, w_hbm, weights_hbm,
    tok_out, gate_out, grad_out,
    xc, part_g, wgu, wdn, dgu, whid, sib_send, sib_recv, pair_send, pair_recv, wacc,
    rz_a, rz_b, rp_a, rp_b,
    loc_sem, bs_sem, br_sem, xs_sem, xr_sem, ls_sem, lr_sem, zs_sem, zr_sem, ps_sem, pr_sem,
    ss_sem, sr_sem, ws_sem, wr_sem, out_sem,
):
    f32, bf16 = jnp.float32, jnp.bfloat16
    z_count = experts // 4
    tok, depth = x_hbm.shape
    ff = weights_hbm.shape[2]
    sections = lax.axis_size("section")
    share = depth // sections
    sec = lax.axis_index("section")
    me = lax.axis_index("expert")
    z, yb, xb = me // 4, (me // 2) % 2, me % 2
    partner = me + 1 - 2 * xb
    peers = {
        "up": {"expert": me + 4},
        "down": {"expert": me - 4},
        "y": {"expert": me + 2 - 4 * yb},
        "x": {"expert": partner},
        "sec": {"section": 1 - sec},
    }
    has = {"up": z < z_count - 1, "down": z > 0, "y": None, "x": None, "sec": None}
    dirs = {"up": 0, "down": 1, "y": 2}
    order_z = line_order(z_count)
    early, late = range(len(cuts) - 1), len(cuts) - 1

    def when(*conds):
        conds = [cond for cond in conds if cond is not None]
        if not conds:
            return lambda body: body()
        joined = conds[0]
        for cond in conds[1:]:
            joined = joined & cond
        return pl.when(joined)

    def slot_of(fp, zz):
        return 2 * zz + (yb + fp) % 2

    own = slot_of(0, z)
    local = [
        pltpu.make_async_copy(x_hbm, xc.at[own, :, pl.ds(0, depth)], loc_sem.at[0]),
        pltpu.make_async_copy(c_hbm, xc.at[own, :, pl.ds(depth, depth)], loc_sem.at[1]),
        pltpu.make_async_copy(w_hbm, xc.at[own, :, pl.ds(2 * depth, LANES)], loc_sem.at[2]),
        pltpu.make_async_copy(weights_hbm.at[0], wgu.at[:, pl.ds(0, ff)], loc_sem.at[3]),
        pltpu.make_async_copy(weights_hbm.at[1], wgu.at[:, pl.ds(ff, ff)], loc_sem.at[4]),
        pltpu.make_async_copy(weights_hbm.at[2], wdn.at[:, pl.ds(0, ff)], loc_sem.at[5]),
    ]
    for copy in local:
        copy.start()

    barrier = pltpu.get_barrier_semaphore()
    for name, peer in peers.items():
        @when(has[name])
        def _(peer=peer):
            pl.semaphore_signal(barrier, inc=1, device_id=peer, device_id_type=MESH)
    pl.semaphore_wait(barrier, 3 + jnp.where(has["up"], 1, 0) + jnp.where(has["down"], 1, 0))

    for copy in local[:3]:
        copy.wait()

    def block_copy(part, slot, name):
        start, rows = cuts[part]
        view = xc.at[slot, pl.ds(start, rows)]
        return pltpu.make_async_remote_copy(
            src_ref=view,
            dst_ref=view,
            send_sem=bs_sem.at[part, dirs[name], slot],
            recv_sem=br_sem.at[part, slot],
            device_id=peers[name],
            device_id_type=MESH,
        )

    block_copy(late, own, "y").start()
    for part in early:
        for name in ("up", "down", "y"):
            @when(has[name])
            def _(part=part, name=name):
                block_copy(part, own, name).start()
    for name in ("up", "down"):
        @when(has[name])
        def _(name=name):
            block_copy(late, own, name).start()

    chunks = wr_sem.shape[0]
    width = share // chunks

    def weight_copies(half, k, name, send_sem, recv_sem, mine):
        rows = pl.ds(pl.multiple_of((half * chunks + k) * width, width), width)
        pairs = (
            (wgu.at[rows, pl.ds(0, 2 * ff)], wgu.at[rows, pl.ds(2 * ff, 2 * ff)]),
            (wdn.at[rows, pl.ds(0, ff)], wdn.at[rows, pl.ds(ff, ff)]),
        )
        return [
            pltpu.make_async_remote_copy(
                src_ref=a if mine else b,
                dst_ref=b,
                send_sem=send_sem.at[k, n],
                recv_sem=recv_sem.at[k, n],
                device_id=peers[name],
                device_id_type=MESH,
            )
            for n, (a, b) in enumerate(pairs)
        ]

    def pair_weights(k):
        return weight_copies(sec, k, "x", xs_sem, xr_sem, True)

    def handed_weights(half, k):
        return weight_copies(half, k, "sec", ls_sem, lr_sem, False)

    for copy in local[3:]:
        copy.wait()
    for k in range(chunks):
        for copy in pair_weights(k):
            copy.start()

    block_copy(late, slot_of(1, z), "y").wait_recv()
    for name in ("up", "down"):
        @when(has[name])
        def _(name=name):
            block_copy(late, slot_of(1, z), name).start()

    lane = lax.broadcasted_iota(jnp.int32, (1, LANES), 1)
    pair = 2
    rows_step = pair * tok

    def inside(zz):
        return (zz >= 0) & (zz < z_count)

    def project(zz, q):
        slot = pair * zz
        expert = jnp.where(q == 0, me, partner)
        gu_cols = pl.ds(pl.multiple_of(q * 2 * ff, 2 * ff), 2 * ff)
        dn_cols = pl.ds(pl.multiple_of(q * ff, ff), ff)
        x = xc[pl.ds(slot, pair), :, pl.ds(0, depth)].reshape(rows_step, depth)
        c = xc[pl.ds(slot, pair), :, pl.ds(depth, depth)].reshape(rows_step, depth)
        w = xc[pl.ds(slot, pair), :, pl.ds(2 * depth, LANES)].reshape(rows_step, LANES)
        weight = jnp.sum(jnp.where(lane == expert, w.astype(f32), 0.0), axis=1, keepdims=True)
        gu = jnp.dot(x, wgu[:, gu_cols], preferred_element_type=f32)
        back = jnp.dot(c, wdn[:, dn_cols], preferred_element_type=f32)
        gate, up = gu[:, :ff], gu[:, ff:]
        sig = jax.nn.sigmoid(gate)
        silu = gate * sig
        hid = silu * up
        row_gate = jnp.sum(hid * back, axis=1, keepdims=True)
        d_hid = weight * back
        d_gate = (d_hid * up * sig * (1.0 + gate * (1.0 - sig))).astype(bf16)
        d_up = (d_hid * silu).astype(bf16)
        rows = pl.ds(pl.multiple_of(slot * tok, rows_step), rows_step)
        dgu[rows, gu_cols] = jnp.concatenate([d_gate, d_up], axis=1)
        whid[rows, dn_cols] = (weight * hid).astype(bf16)
        marked = jnp.where(lane == expert, row_gate, 0.0).astype(bf16).reshape(pair, tok, LANES)
        gates = (pl.ds(slot, pair), slice(None), pl.ds(depth, LANES))

        @pl.when(q == 0)
        def _():
            part_g[gates] = marked

        @pl.when(q == 1)
        def _():
            part_g[gates] = part_g[gates] + marked
            grads = lax.dot_general(
                dgu[rows, :], wgu[...], (((1,), (1,)), ((), ())), preferred_element_type=f32
            )
            part_g[pl.ds(slot, pair), :, pl.ds(0, depth)] = grads.astype(bf16).reshape(pair, tok, depth)

    swap_step = min(2, z_count)
    ways = ((-1, "up"), (1, "down"))

    def step(st, carry):
        @pl.when(st < z_count)
        def _():
            for part in early:
                for sign, onward in ways:
                    zz = z + sign * st

                    @pl.when(inside(zz))
                    def _(part=part, zz=zz, onward=onward):
                        block_copy(part, slot_of(0, zz), "y").wait_recv()

                        @when(has[onward])
                        def _():
                            block_copy(part, slot_of(0, zz), onward).start()

                        block_copy(part, slot_of(0, zz), "y").start()
            for sign, onward in ways:
                zz = z + sign * st

                @pl.when(inside(zz))
                def _(zz=zz, onward=onward):
                    for fp in (0, 1):
                        block_copy(late, slot_of(fp, zz), "y").wait_recv()

                        @when(has[onward])
                        def _(fp=fp):
                            block_copy(late, slot_of(fp, zz), onward).start()

        low = jnp.maximum(2 * st - 3, 0)
        count = 2 * st - 1 - low
        low_pair = jnp.where(st == swap_step, 0, low)
        count_pair = jnp.where(st < swap_step, 0, 2 * st - 1 - low_pair)

        def item(n, inner):
            q = jnp.where(n < count, 0, 1)
            place = jnp.where(n < count, low + n, low_pair + n - count)
            zz = z + ((place + 1) // 2) * (1 - 2 * (place % 2))

            @pl.when((n == count) & (st == swap_step))
            def _():
                for k in range(chunks):
                    for copy in pair_weights(k):
                        copy.wait_recv()
                    for copy in handed_weights(sec, k):
                        copy.start()
                for k in range(chunks):
                    for copy in handed_weights(1 - sec, k):
                        copy.wait_recv()

            @pl.when(inside(zz))
            def _():
                @pl.when(q == 0)
                def _():
                    for part in early:
                        block_copy(part, slot_of(1, zz), "y").wait_recv()

                project(zz, q)

            return inner

        lax.fori_loop(0, count + count_pair, item, 0)
        return carry

    lax.fori_loop(1, z_count + 1, step, 0)

    halves = ((0, split), (split, tok - split))

    def add_rows(slot, start, rows, view):
        def strip(k, carry):
            at = pl.ds(pl.multiple_of(start + k * ROW_TILE, ROW_TILE), ROW_TILE)
            off = pl.ds(pl.multiple_of(k * ROW_TILE, ROW_TILE), ROW_TILE)
            total = part_g[slot, at, :].astype(f32) + view[off, :].astype(f32)
            part_g[slot, at, :] = total.astype(bf16)
            return carry

        lax.fori_loop(0, rows // ROW_TILE, strip, 0)

    def p_copy(part, zz, slot):
        start, rows = halves[part]
        place = zz if part == 0 else z_count
        return pltpu.make_async_remote_copy(
            src_ref=part_g.at[slot, pl.ds(start, rows)],
            dst_ref=rp_a.at[zz] if part == 0 else rp_b,
            send_sem=ps_sem.at[place],
            recv_sem=pr_sem.at[place],
            device_id=peers["y"],
            device_id_type=MESH,
        )

    groups = ((0, 0, rz_a), (1, 0, rz_b.at[0]), (1, 1, rz_b.at[1]))

    def z_copy(group, dest, name, place):
        part, fp, buf = groups[group]
        start, rows = halves[part]
        return pltpu.make_async_remote_copy(
            src_ref=part_g.at[slot_of(fp, dest), pl.ds(start, rows)],
            dst_ref=buf.at[place],
            send_sem=zs_sem.at[group, dest],
            recv_sem=zr_sem.at[group, place],
            device_id=peers[name],
            device_id_type=MESH,
        )

    def z_take(group, dest, place):
        part, fp, buf = groups[group]
        start, rows = halves[part]
        z_copy(group, 0, "y", place).wait_recv()
        add_rows(slot_of(fp, dest), start, rows, buf.at[place])

    def z_send(group, dest):
        @pl.when(z < dest)
        def _():
            z_copy(group, dest, "up", dest).start()

        @pl.when(z > dest)
        def _():
            z_copy(group, dest, "down", jnp.where(z == dest + 1, z_count, dest)).start()

    def relays(dest):
        return ((z < dest) & (z > 0)) | ((z > dest) & (z < z_count - 1))

    def z_origin(group, dest):
        @pl.when(jnp.logical_not(relays(dest)))
        def _():
            z_send(group, dest)

    def z_relay(group, dest):
        @pl.when(relays(dest))
        def _():
            z_take(group, dest, dest)
            z_send(group, dest)

    def z_own(group):
        @pl.when(z > 0)
        def _():
            z_take(group, z, z)

        @pl.when(z < z_count - 1)
        def _():
            z_take(group, z, z_count)

    def chunk_rows(k):
        return pl.ds(pl.multiple_of(k * width, width), width)

    def out_copy(k):
        at = chunk_rows(k)
        return pltpu.make_async_copy(wacc.at[:, at, :], grad_out.at[:, at, :], out_sem.at[k])

    def chunk_copy(k, src, dst, send_sem, recv_sem, name):
        return pltpu.make_async_remote_copy(
            src_ref=src.at[chunk_rows(k)],
            dst_ref=dst.at[chunk_rows(k)],
            send_sem=send_sem.at[k],
            recv_sem=recv_sem.at[k],
            device_id=peers[name],
            device_id_type=MESH,
        )

    def sib_copy(k):
        return chunk_copy(k, sib_send, sib_recv, ss_sem, sr_sem, "sec")

    def pair_copy(k):
        return chunk_copy(k, pair_send, pair_recv, ws_sem, wr_sem, "x")

    fold = (((0,), (0,)), ((), ()))

    for zz in order_z:
        p_copy(0, zz, slot_of(1, zz)).start()
        z_origin(2, zz)
        z_origin(1, zz)

    def returned(i, carry):
        @pl.when(i < 2 * chunks)
        def _():
            k = i // 2
            away = i % 2 == 0
            half = jnp.where(away, 1 - sec, sec)
            col = (half * chunks + k) * width
            xs = xc[:, :, pl.ds(pl.multiple_of(col, width), width)].reshape(-1, width)
            cs = xc[:, :, pl.ds(pl.multiple_of(depth + col, width), width)].reshape(-1, width)
            got_gu = lax.dot_general(xs, dgu[...], fold, preferred_element_type=f32)
            got_dn = lax.dot_general(cs, whid[...], fold, preferred_element_type=f32)

            @pl.when(away)
            def _():
                sib_send[chunk_rows(k), pl.ds(0, 4 * ff)] = got_gu.astype(bf16)
                sib_send[chunk_rows(k), pl.ds(4 * ff, 2 * ff)] = got_dn.astype(bf16)
                sib_copy(k).start()

            @pl.when(jnp.logical_not(away))
            def _():
                sib_copy(k).wait_recv()
                all_gu = got_gu + sib_recv[chunk_rows(k), pl.ds(0, 4 * ff)].astype(f32)
                all_dn = got_dn + sib_recv[chunk_rows(k), pl.ds(4 * ff, 2 * ff)].astype(f32)
                pair_send[chunk_rows(k), pl.ds(0, 2 * ff)] = all_gu[:, 2 * ff:].astype(bf16)
                pair_send[chunk_rows(k), pl.ds(2 * ff, ff)] = all_dn[:, ff:].astype(bf16)
                pair_copy(k).start()
                wacc[0, chunk_rows(k), :] = all_gu[:, :ff]
                wacc[1, chunk_rows(k), :] = all_gu[:, ff : 2 * ff]
                wacc[2, chunk_rows(k), :] = all_dn[:, :ff]

        turn = (i - 3) // 2

        @pl.when((i >= 3) & (i % 2 == 1))
        def _():
            dest = pick(order_z, turn)

            @pl.when(turn == 0)
            def _():
                for zz in order_z:
                    z_relay(2, zz)
                    z_relay(1, zz)

            p_copy(0, dest, own).wait_recv()
            add_rows(slot_of(0, dest), 0, split, rp_a.at[dest])
            z_origin(0, dest)

            @pl.when(turn >= 1)
            def _():
                z_relay(0, pick(order_z, (turn + z_count - 1) % z_count))

            @pl.when(turn == z_count - 2)
            def _():
                z_own(2)
                p_copy(1, z, slot_of(1, z)).start()

        return carry

    lax.fori_loop(0, max(2 * chunks, 2 * z_count + 2), returned, 0)

    z_relay(0, order_z[-1])
    p_copy(1, z, own).wait_recv()
    add_rows(own, split, tok - split, rp_b)
    z_own(1)
    z_own(0)
    token_copies = (
        pltpu.make_async_copy(part_g.at[own, :, pl.ds(0, depth)], tok_out, loc_sem.at[0]),
        pltpu.make_async_copy(part_g.at[own, :, pl.ds(depth, LANES)], gate_out, loc_sem.at[1]),
    )
    for copy in token_copies:
        copy.start()

    def finish(k, carry):
        pair_copy(k).wait_recv()
        for m in range(3):
            other = pair_recv[chunk_rows(k), pl.ds(m * ff, ff)].astype(f32)
            wacc[m, chunk_rows(k), :] = (wacc[m, chunk_rows(k), :] + other) / sections
        out_copy(k).start()
        return carry

    lax.fori_loop(0, chunks, finish, 0)

    for copy in token_copies:
        copy.wait()
    for k in range(chunks):
        out_copy(k).wait()
        sib_copy(k).wait_send()
        pair_copy(k).wait_send()
        for copy in pair_weights(k):
            copy.wait_send()
        for copy in handed_weights(sec, k):
            copy.wait_send()
    block_copy(late, own, "y").wait_send()
    for name in ("up", "down"):
        @when(has[name])
        def _(name=name):
            for part in (*early, late):
                block_copy(part, own, name).wait_send()
            block_copy(late, slot_of(1, z), name).wait_send()
    for part in early:
        block_copy(part, own, "y").wait_send()

    def drain(st, carry):
        for sign, onward in ways:
            zz = z + sign * st

            @pl.when(inside(zz))
            def _(zz=zz, onward=onward):
                for part in early:
                    block_copy(part, slot_of(0, zz), "y").wait_send()

                @when(has[onward])
                def _():
                    for part in early:
                        block_copy(part, slot_of(0, zz), onward).wait_send()
                    for fp in (0, 1):
                        block_copy(late, slot_of(fp, zz), onward).wait_send()

        return carry

    lax.fori_loop(1, z_count, drain, 0)
    for zz in range(z_count):
        p_copy(0, zz, own).wait_send()
    p_copy(1, z, own).wait_send()
    for group in range(3):
        for dest in range(z_count):
            @pl.when(z != dest)
            def _():
                z_copy(group, dest, "y", dest).wait_send()


def gathered(tokens, cotangent, routes, route_weights, weights):
    experts = lax.axis_size("expert")
    sections = lax.axis_size("section")
    z_count = experts // 4
    blocks = 2 * z_count
    tok, depth = tokens.shape[1:]
    ff = weights.shape[3]
    named = routes[0][:, :, None] == jnp.arange(LANES, dtype=jnp.int32)
    dense_w = jnp.sum(jnp.where(named, route_weights[0][:, :, None], 0), axis=1)
    unit = tok // 8 // ROW_TILE * ROW_TILE
    split = 7 * unit
    cuts = ((0, 4 * unit), (4 * unit, 3 * unit), (split, tok - split))
    bf16 = jnp.bfloat16
    g_width = depth + LANES
    share = depth // sections
    chunks = max(1, share // 256)
    dma = pltpu.SemaphoreType.DMA
    any_spec = pl.BlockSpec(memory_space=pl.ANY)
    token_grads, gates, grads = pl.pallas_call(
        functools.partial(fused_kernel, experts, split, cuts),
        out_shape=(
            jax.ShapeDtypeStruct((tok, depth), bf16),
            jax.ShapeDtypeStruct((tok, LANES), bf16),
            jax.ShapeDtypeStruct((3, share, ff), jnp.float32),
        ),
        in_specs=[any_spec] * 4,
        out_specs=(any_spec,) * 3,
        scratch_shapes=[
            pltpu.VMEM((blocks, tok, 2 * depth + LANES), bf16),
            pltpu.VMEM((blocks, tok, g_width), bf16),
            pltpu.VMEM((depth, 4 * ff), bf16),
            pltpu.VMEM((depth, 2 * ff), bf16),
            pltpu.VMEM((blocks * tok, 4 * ff), bf16),
            pltpu.VMEM((blocks * tok, 2 * ff), bf16),
            pltpu.VMEM((share, 6 * ff), bf16),
            pltpu.VMEM((share, 6 * ff), bf16),
            pltpu.VMEM((share, 3 * ff), bf16),
            pltpu.VMEM((share, 3 * ff), bf16),
            pltpu.VMEM((3, share, ff), jnp.float32),
            pltpu.VMEM((z_count + 1, split, g_width), bf16),
            pltpu.VMEM((2, z_count + 1, tok - split, g_width), bf16),
            pltpu.VMEM((z_count, split, g_width), bf16),
            pltpu.VMEM((tok - split, g_width), bf16),
            dma((6,)),
            dma((len(cuts), 3, blocks)),
            dma((len(cuts), blocks)),
            dma((chunks, 2)),
            dma((chunks, 2)),
            dma((chunks, 2)),
            dma((chunks, 2)),
            dma((3, z_count)),
            dma((3, z_count + 1)),
            dma((z_count + 1,)),
            dma((z_count + 1,)),
            dma((chunks,)),
            dma((chunks,)),
            dma((chunks,)),
            dma((chunks,)),
            dma((chunks,)),
        ],
        compiler_params=pltpu.CompilerParams(
            collective_id=0, has_side_effects=True, vmem_limit_bytes=67043328
        ),
    )(tokens[0], cotangent[0], dense_w, weights[:, 0])
    gate_grads = jnp.sum(jnp.where(named, gates[:, None, :], 0), axis=2)[None]
    return (token_grads[None], gate_grads, grads[:, None])


def exchanged(tokens, cotangent, routes, route_weights, weights):
    experts = lax.axis_size("expert")
    tok_count, depth = tokens.shape[1:]
    top_k = routes.shape[-1]
    capacity = min(tok_count, max(2, (9 * tok_count * top_k + 8 * experts - 1) // (8 * experts)))
    route_block = routes[0]
    slots, slot_table = slot_assign(route_block, experts, capacity)
    token_ix = slot_table // top_k
    zero_row = jnp.zeros((1, depth), tokens.dtype)
    send_in = jnp.concatenate([tokens[0], zero_row])[token_ix]
    send_cot = jnp.concatenate([cotangent[0], zero_row])[token_ix]
    send_weight = jnp.concatenate(
        [route_weights[0].reshape(-1), jnp.zeros((1,), route_weights.dtype)]
    )[slot_table]
    recv_in, recv_cot, recv_weight = (
        lax.all_to_all(block, "expert", split_axis=0, concat_axis=0, tiled=True)
        for block in (send_in, send_cot, send_weight)
    )
    row_gate, row_grads, weight_part = expert_math(
        recv_in.reshape(-1, depth), recv_cot.reshape(-1, depth), recv_weight.reshape(-1), weights[:, 0]
    )
    back_rows, back_gate = (
        lax.all_to_all(block, "expert", split_axis=0, concat_axis=0, tiled=True)
        for block in (
            row_grads.reshape(experts, capacity, depth),
            row_gate.reshape(experts, capacity),
        )
    )
    flat_rows = back_rows.reshape(experts * capacity, depth)
    flat_index = route_block * capacity + slots
    accum = jnp.zeros((tok_count, depth), jnp.float32)
    for position in range(top_k):
        accum = accum + flat_rows[flat_index[:, position]].astype(jnp.float32)
    token_grads = accum.astype(jnp.bfloat16)[None]
    gate_grads = back_gate.reshape(-1)[flat_index][None]
    return (token_grads, gate_grads, section_mean(weight_part))


def solution(mesh):
    placed = P("section", "expert", None)

    def per_device(tokens, cotangent, routes, route_weights, weights):
        dense = 4 * routes.shape[-1] >= lax.axis_size("expert")
        plan = gathered if dense else exchanged
        return plan(tokens, cotangent, routes, route_weights, weights)

    return jax.shard_map(
        per_device,
        mesh=mesh,
        in_specs=(placed, placed, placed, placed, P(None, "expert", None, None)),
        out_specs=(placed, placed, P(None, "expert", "section", None)),
        check_vma=False,
    )
```

time: 241 us -> 182 us (0.76)
  the two profiles are of different devices: /device:TPU:8 before, /device:TPU:0 now
where the time goes in v1:
time: 182 us
  Pallas kernels  169 us (93%)
  local copies, waits for them, and re-layouts  9.57 us (5%)
  other arithmetic  2.19 us (1%)
    pallas_call x1, Pallas kernels, gathered(): pl.pallas_call(functools.partial(fused_kernel, experts, split, cuts), out...  169 us
    unnamed x5, local copies, waits for them, and re-layouts  7.98 us

profile of v1, /device:TPU:0, one launch (start us, length us, event | category | flops | bytes accessed | tf_op | source)
XLA Modules:
  0.0 181.9 jit_solution(8064301291974453983)
XLA Ops:
  0.6 0.8 copy.12
  1.4 0.8 copy.11
  2.2 0.0 copy-start
  2.2 0.6 copy-done
  2.8 1.0 fusion.2.w_hbm
  3.8 169.4 %shard_map.76 = (bf16[128,2048]{1,0:T(8,128)(2,1)}, bf16[128,128]{1,0:T(8,128)(2,1)}, f32[3,1024,384]{2,1,0:T(8,128)}) custom-call(bf16[128,2048]{1,0:T(8,128)(2,1)} %bitcast.13, bf16[128,2048]{1,0:T(8,128)(2,1)} %bitcast.14, bf16[128,128]{1,0:T(8,128)(2,1)} %fusion.2.w_hbm, bf16[3,2048,384]{2,1,0:T(8,128)(2,1)} %bitcast.10), custom_call_target="tpu_custom_call" | custom-call | tf_op jit(solution)/shard_map/pallas_call | solution.py:574
  173.3 1.2 fusion.3
  174.5 0.7 copy.13
  175.2 1.9 %copy.17 = bf16[1,128,2048]{2,1,0:T(8,128)(2,1)} copy(bf16[1,128,2048]{2,1,0:T(8,128)(2,1)} %bitcast.12) | data formatting | bytes 1048576
  177.0 4.8 %copy.18 = f32[3,1,1024,384]{3,2,1,0:T(8,128)} copy(f32[3,1,1024,384]{3,2,1,0:T(8,128)} %bitcast.11) | data formatting | bytes 9437184
Async XLA Ops:
  2.2 0.6 copy-start
